TPU v7x, 32 devices: a whole 2x2x4 slice. The times are simulated.
32 devices in a mesh: ma: 8 (over z, y), row: 4 (over x, core).
Axes of the slice: x: 2, y: 2, z: 4, core: 2. Of those that a mesh axis runs over, the one named last changes fastest.
Arguments:
- velocity: bfloat16 [3, 2, 16, 32, 65], P(None, None, 'row', 'ma'), may hold values from -6 to 6
- vorticity: bfloat16 [3, 2, 16, 32, 65], P(None, None, 'row', 'ma'), may hold values from -6 to 6
- legendre: bfloat16 [32, 65, 384], P('ma'), may hold values from -0.75 to 0.75
- pair_order: int32 [32], P('ma'), may hold values from 0 to 31, each once
- lat_weight: float32 [384], replicated, may hold values from 0.5 to 2
- diffusivity: float32 [16], replicated, may hold values from 0.25 to 2.5
Outputs:
- new_velocity: float32 [3, 2, 16, 32, 65], P(None, None, 'row', 'ma')
Inputs may be any that keep to these rules, and one draw needn't show every extreme that they name: pair_order holds each of 0 to 31 exactly once.
All inputs are finite; a program needn't handle non-finite values.
Results may differ from a plain program's by a relative error of at most 0.0095.
Values may be sent and summed in bfloat16 or wider, within the bound.
A program may use at most 128 MiB of HBM per device.

v0:
```python
import functools
import math

import jax
import jax.numpy as jnp
import numpy as np
from jax import lax
from jax.experimental import pallas as pl
from jax.experimental.pallas import tpu as pltpu
from jax.sharding import PartitionSpec as P

NLON = 2048


STEP_SIZE = 1.0


def with_halo(cells, sides, width):
    for axis, dim in sides:
        count = lax.axis_size(axis)
        ends = count - 1
        head = lax.slice_in_dim(cells, 0, width, axis=dim)
        tail = lax.slice_in_dim(cells, cells.shape[dim] - width, cells.shape[dim], axis=dim)
        cells = jnp.concatenate(
            [
                lax.ppermute(tail, axis, [(i, (i + 1) % count) for i in range(ends)]),
                cells,
                lax.ppermute(head, axis, [((i + 1) % count, i) for i in range(ends)]),
            ],
            axis=dim,
        )
    return cells


def row_masks(low_order, pack_rows):
    orders_all = pack_rows - 1
    row_index = jnp.arange(pack_rows, dtype=jnp.int32)[None, :]
    low_column = low_order[:, None]
    is_lower = row_index < orders_all - low_column
    not_lower = jnp.logical_not(is_lower)
    even_low = row_index % 2 == 0
    even_high = (row_index + low_column) % 2 == 0
    low_pair = jnp.stack([is_lower & even_low, is_lower & jnp.logical_not(even_low)])
    high_pair = jnp.stack([not_lower & even_high, not_lower & jnp.logical_not(even_high)])
    return jnp.stack([low_pair, high_pair])


def cross_product(velocity_grid, vorticity_grid):
    return jnp.stack(
        [
            velocity_grid[1] * vorticity_grid[2] - velocity_grid[2] * vorticity_grid[1],
            velocity_grid[2] * vorticity_grid[0] - velocity_grid[0] * vorticity_grid[2],
            velocity_grid[0] * vorticity_grid[1] - velocity_grid[1] * vorticity_grid[0],
        ]
    )


def lon_table(column_order, is_imag, lon_start, lon_count):
    lon_index = lon_start + jnp.arange(lon_count, dtype=jnp.int32)
    angle_index = column_order[:, None] * lon_index[None, :] % NLON
    angle_value = angle_index.astype(jnp.float32) * (2.0 * math.pi / NLON)
    return jnp.where(is_imag[:, None], -jnp.sin(angle_value), jnp.cos(angle_value))


def local(velocity, vorticity, legendre, pair_order, lat_weight, diffusivity):
    pair_count = pair_order.shape[0]
    pack_rows = legendre.shape[1]
    half_lat = legendre.shape[2]
    nlat_all = 2 * half_lat
    levels_dev = velocity.shape[2]
    orders_all = pack_rows - 1
    inv_orders = 1.0 / math.sqrt(orders_all)
    inv_lon = 1.0 / math.sqrt(NLON)
    lon_width = NLON // 4
    mask_bool = row_masks(pair_order, pack_rows)
    fields = jnp.concatenate([velocity, vorticity], axis=0)
    masked = fields[None, None] * mask_bool.astype(jnp.bfloat16)[:, :, None, None, None]
    halves = jnp.einsum(
        "oqfilsr,srj->qfliosj", masked, legendre, preferred_element_type=jnp.float32
    )
    north_part = halves[0] + halves[1]
    south_part = halves[0] - halves[1]
    both_parts = jnp.concatenate([north_part, south_part], axis=-1)
    spectral = jnp.transpose(both_parts, (0, 1, 5, 2, 3, 4))
    spectral = spectral.reshape(6, levels_dev, nlat_all, 4 * pair_count).astype(jnp.bfloat16)
    gathered_ids = lax.all_gather(pair_order, "ma", axis=0, tiled=True)
    pair_slots = gathered_ids.reshape(-1, 1, 1, pair_count)
    both_orders = jnp.concatenate([pair_slots, orders_all - 1 - pair_slots], axis=2)
    full_shape = (both_orders.shape[0], 2, 2, pair_count)
    column_order = jnp.broadcast_to(both_orders, full_shape).reshape(-1)
    part_index = jnp.arange(2, dtype=jnp.int32)[None, :, None, None]
    is_imag = jnp.broadcast_to(part_index, full_shape).reshape(-1) == 1
    tables = [
        lon_table(column_order, is_imag, lon_block * lon_width, lon_width).astype(jnp.bfloat16)
        for lon_block in range(4)
    ]
    spec_block = lax.all_to_all(spectral, "ma", split_axis=2, concat_axis=3, tiled=True)
    accumulated = jnp.zeros((3,) + spec_block.shape[1:], jnp.float32)
    for lon_block in range(4):
        table_block = tables[lon_block]
        grid_values = (
            jnp.einsum("flac,cb->flab", spec_block, table_block, preferred_element_type=jnp.float32)
            * inv_orders
        )
        lamb_vector = cross_product(grid_values[:3], grid_values[3:])
        accumulated = accumulated + jnp.einsum(
            "flab,cb->flac",
            lamb_vector,
            table_block.astype(jnp.float32),
            precision=lax.Precision.HIGH,
            preferred_element_type=jnp.float32,
        )
    lamb_spec = (accumulated * inv_lon).astype(jnp.bfloat16)
    selector = jnp.transpose(mask_bool.astype(jnp.float32), (1, 0, 2, 3))[:, None, None, None]
    lamb_block = lax.all_to_all(lamb_spec, "ma", split_axis=3, concat_axis=2, tiled=True)
    item_count = lamb_block.shape[0]
    shaped = lamb_block.astype(jnp.float32).reshape(
        item_count, levels_dev, nlat_all, 2, 2, pair_count
    )
    shaped = jnp.transpose(shaped, (0, 1, 3, 4, 5, 2))
    north_side = shaped[..., :half_lat]
    south_side = shaped[..., half_lat:]
    weighted = jnp.stack(
        [lat_weight * (north_side + south_side), lat_weight * (north_side - south_side)]
    )
    weighted = weighted.astype(jnp.bfloat16)
    projected = jnp.einsum(
        "qfliosj,srj->qfliosr", weighted, legendre, preferred_element_type=jnp.float32
    )
    picked = jnp.sum(projected * selector, axis=(0, 4))
    tendency = jnp.transpose(picked, (0, 2, 1, 3, 4))
    source = velocity.astype(jnp.float32) + STEP_SIZE * tendency
    row_start = lax.axis_index("row") * levels_dev
    level_total = levels_dev * lax.axis_size("row")
    extended = with_halo(source.astype(jnp.bfloat16), (("row", 2),), 2).astype(source.dtype)
    padded_coupling = jnp.pad(diffusivity, (2, 2))
    wide_coupling = lax.dynamic_slice_in_dim(padded_coupling, row_start, levels_dev + 4)[
        None, None, :, None, None
    ]
    inner_coupling = wide_coupling[:, :, 1:-1]
    first_wide = (
        extended[:, :, 1:-1] + inner_coupling * (extended[:, :, :-2] + extended[:, :, 2:])
    ) / (1.0 + 2.0 * inner_coupling)
    global_level = row_start - 1 + jnp.arange(levels_dev + 2, dtype=jnp.int32)
    inside = ((global_level >= 0) & (global_level < level_total)).astype(jnp.float32)
    first_wide = first_wide * inside[None, None, :, None, None]
    own_coupling = wide_coupling[:, :, 2:-2]
    return (source + own_coupling * (first_wide[:, :, :-2] + first_wide[:, :, 2:])) / (
        1.0 + 2.0 * own_coupling
    )

def lon_count(orders_all):
    need = 3 * (orders_all - 1) + 1
    return min(NLON, -(-need // 64) * 64)


def remote(src, dst, send_sem, recv_sem, device_id):
    return pltpu.make_async_remote_copy(
        src_ref=src,
        dst_ref=dst,
        send_sem=send_sem,
        recv_sem=recv_sem,
        device_id=device_id,
        device_id_type=pl.DeviceIdType.MESH,
    )


def fused_kernel(
    n_ma, n_row, pairs, rows, levels, scale,
    velocity_hbm, vorticity_hbm, legendre_hbm, order_hbm, weight_hbm, dif_hbm, tab_hbm, tab_t_hbm,
    out_ref,
    velocity_ref, vorticity_ref, legendre_ref, order_ref, weight_ref, dif_ref, tab_ref, tab_t_ref, load_sem,
    leg_rows, leg_ref, rest_ref, coef_all, leg_all, rest_all, rest_t, onehot, ops, spec, wgt, part, part_in, ext, halo,
    coef_send, coef_recv, leg_send, leg_recv, swap_send, swap_recv, rest_send, rest_recv, part_send, part_recv, halo_send, halo_recv,
):
    me = lax.axis_index("ma")
    row = lax.axis_index("row")
    _, chunks, groups, wide = coef_all.shape
    coef_ref = coef_all.at[0]
    lanes = (chunks + 1) * wide
    fields2 = groups // 2
    orders = rows - 1
    slots = 2 * pairs
    full = n_ma * slots
    lat = leg_ref.shape[2]
    side = wide // 2
    main = pairs * orders
    per_chunk = pairs // chunks
    f32 = jnp.float32
    bf16 = jnp.bfloat16
    n_z = n_ma // 2
    z, y = me // 2, lax.rem(me, 2)
    half = lax.rem(row, 2)
    mate_row = row + 1 - 2 * half

    def target(s):
        return lax.rem(z + s // 2, n_z) * 2 + lax.rem(y + lax.rem(s, 2), 2)

    def origin(s):
        return lax.rem(z + n_z - s // 2, n_z) * 2 + lax.rem(y + lax.rem(s, 2), 2)

    left = lax.rem(row + n_row - 1, n_row)
    right = lax.rem(row + 1, n_row)

    barrier = pltpu.get_barrier_semaphore()
    for d in range(1, n_ma):
        pl.semaphore_signal(
            barrier, inc=1, device_id=(lax.rem(me + d, n_ma), row), device_id_type=pl.DeviceIdType.MESH
        )
    for beside in (left, right):
        pl.semaphore_signal(barrier, inc=1, device_id=(me, beside), device_id_type=pl.DeviceIdType.MESH)

    loads = [
        pltpu.make_async_copy(src, dst, load_sem.at[i])
        for i, (src, dst) in enumerate(
            [
                (legendre_hbm, legendre_ref),
                (velocity_hbm, velocity_ref),
                (vorticity_hbm, vorticity_ref),
                (order_hbm, order_ref),
                (weight_hbm, weight_ref),
                (dif_hbm, dif_ref),
                (tab_hbm, tab_ref),
                (tab_t_hbm, tab_t_ref),
            ]
        )
    ]
    for load in loads:
        load.start()
    for load in loads[:4]:
        load.wait()

    for r in range(rows):
        values = legendre_ref[r].astype(f32)
        for t in range(leg_rows.shape[0]):
            leg_rows[t, r * pairs : (r + 1) * pairs, :] = values[:, t * wide : (t + 1) * wide]
    packs = [
        jnp.concatenate([velocity_ref[...].astype(f32)[:, p], vorticity_ref[...].astype(f32)[:, p]], axis=0)
        for p in range(pairs)
    ]
    column = lax.broadcasted_iota(jnp.int32, (groups, wide), 1)
    ends = jnp.zeros((groups, wide), f32)
    for p in range(pairs):
        ends = jnp.where(column == p, packs[p][:, orders:], ends)
    ends = jnp.concatenate([ends, jnp.zeros((wide - groups, wide), f32)], axis=0)
    ends = jnp.transpose(ends)[0:pairs, 0:side]
    tails = jnp.concatenate([leg_rows[t, main : main + pairs, :] for t in range(leg_rows.shape[0])], axis=1)
    order_rows = [jnp.full((1, wide), order_ref[p].astype(f32)) for p in range(pairs)]
    filler = jnp.zeros((pairs, side - lat), f32)
    for b in range(n_ma):
        data_rows = jnp.concatenate([ends, tails[:, b * lat : (b + 1) * lat], filler], axis=1)
        rest_ref[b] = jnp.concatenate([data_rows] + order_rows, axis=0).astype(bf16)
    for c in range(chunks):
        members = range(c * per_chunk, (c + 1) * per_chunk)
        coef_all[0, c] = jnp.concatenate([packs[p][:, :orders] for p in members], axis=1).astype(bf16)
        turned = jnp.concatenate(
            [
                jnp.transpose(
                    jnp.concatenate([leg_rows[t, pl.ds(p, orders, stride=pairs), :] for p in members], axis=0)
                )
                for t in range(leg_rows.shape[0])
            ],
            axis=0,
        ).astype(bf16)
        for b in range(n_ma):
            leg_ref[b, c] = turned[b * lat : (b + 1) * lat]

    pl.semaphore_wait(barrier, n_ma + 1)

    def coef_copy(s):
        return remote(coef_ref, coef_all.at[s], coef_send.at[s], coef_recv.at[s], (target(s), row))

    def leg_copy(s):
        peer = target(s)
        return remote(
            leg_ref.at[peer, half], leg_all.at[s, half], leg_send.at[s], leg_recv.at[s], (peer, row)
        )

    def swap_copy(s):
        return remote(
            leg_all.at[s, half], leg_all.at[s, half], swap_send.at[s], swap_recv.at[s], (me, mate_row)
        )

    def swap_arrival(s):
        return remote(
            leg_all.at[s, half], leg_all.at[s, 1 - half], swap_send.at[s], swap_recv.at[s], (me, mate_row)
        )

    def rest_copy(s):
        peer = target(s)
        return remote(rest_ref.at[peer], rest_all.at[s], rest_send.at[s], rest_recv.at[s], (peer, row))

    far_first = sorted(range(1, n_ma), key=lambda s: (-min(s // 2, n_z - s // 2), -(s % 2)))
    near_first = far_first[::-1]
    for s in far_first:
        rest_copy(s).start()
    for s in far_first:
        leg_copy(s).start()
    for s in far_first:
        coef_copy(s).start()

    leg_all[0] = leg_ref[me]
    rest_all[0] = rest_ref[me]

    def clear(d, carry):
        ops[d] = jnp.zeros(ops.shape[1:], bf16)
        return carry

    lax.fori_loop(0, n_ma, clear, 0)
    for load in loads[4:]:
        load.wait()
    weight = jnp.zeros((1, lat), f32)
    for b in range(n_ma):
        weight = jnp.where(me == b, weight_ref[...].reshape(1, -1)[:, b * lat : (b + 1) * lat], weight)
    weight = weight * scale
    gap = jnp.zeros((1, side - lat), f32)
    weight = jnp.concatenate([weight, gap, weight, gap] * 2, axis=1)

    lane = lax.broadcasted_iota(jnp.int32, (pairs, wide), 1)
    sub = lax.broadcasted_iota(jnp.int32, (pairs, wide), 0)
    m_lane = lax.broadcasted_iota(jnp.int32, (slots, orders), 1)
    m_sub = lax.broadcasted_iota(jnp.int32, (slots, orders), 0)
    lane_row = lane % orders
    own = lane // orders == sub % per_chunk

    def low_orders(d):
        return rest_all[d].astype(f32)[pairs:].astype(jnp.int32)

    def place(d):
        low = low_orders(d)
        order = jnp.zeros((slots, orders), jnp.int32)
        for p in range(pairs):
            value = low[p : p + 1, 0:1]
            order = jnp.where(m_sub == 2 * p, value, order)
            order = jnp.where(m_sub == 2 * p + 1, orders - 1 - value, order)
        onehot[d * slots : (d + 1) * slots, :] = (m_lane == order).astype(f32)

    def synth(d):
        low = low_orders(d)
        lower = lane_row < orders - low
        north_low = (own & lower).astype(f32)
        north_high = (own & jnp.logical_not(lower)).astype(f32)
        south_low = north_low * (1 - 2 * (lane_row & 1)).astype(f32)
        south_high = north_high * (1 - 2 * ((lane_row + low) & 1)).astype(f32)
        north_end = (lane == 8 * d + sub).astype(f32)
        south_end = north_end * (1 - 2 * (low & 1)).astype(f32)
        end_leg = rest_t[side : side + lat, :]
        end_coef = rest_t[0:groups, :].astype(bf16)
        for p in range(pairs):
            c = p // per_chunk
            table = leg_all[d, c].astype(f32)
            at = p * 2 * wide
            for i, factor in enumerate((north_low, south_low, north_high, south_high)):
                ops[d, at + i * side : at + i * side + lat, 0:wide] = (table * factor[p : p + 1]).astype(bf16)
            for i, factor in enumerate((north_end, south_end)):
                first = at + wide + i * side
                ops[d, first : first + lat, wide : 2 * wide] = (end_leg * factor[p : p + 1]).astype(bf16)
            lhs = jnp.concatenate([coef_all[d, c], end_coef], axis=1)
            made = lax.dot_general(
                lhs, ops[d, at : at + 2 * wide, :], (((1,), (1,)), ((), ())), preferred_element_type=f32
            )
            for i in range(2):
                spec[pl.ds(d * slots + 2 * p + i, groups, stride=full), :] = made[:, i * wide : (i + 1) * wide]

    for s in near_first:
        rest_copy(s).wait_recv()
    rest = rest_all[...].astype(f32).reshape(n_ma * 8, wide)
    rest = jnp.concatenate([rest, jnp.zeros((wide - n_ma * 8, wide), f32)], axis=0)
    rest_t[...] = jnp.transpose(rest)
    for d in range(n_ma):
        place(d)
    hot = onehot[...].astype(bf16)
    to_grid = jnp.concatenate(
        [
            lax.dot_general(tab_t_ref[c], hot, (((1,), (1,)), ((), ())), preferred_element_type=f32)
            for c in range(2)
        ],
        axis=1,
    ).astype(bf16)
    to_spec = jnp.concatenate(
        [jnp.dot(hot, tab_ref[c], preferred_element_type=f32) for c in range(2)], axis=0
    ).astype(bf16)
    synth(0)
    for s in near_first:
        leg_copy(s).wait_recv()
        swap_copy(s).start()
    for s in near_first:
        coef_copy(s).wait_recv()
        swap_arrival(s).wait_recv()
        synth(s)

    def middle(j, carry):
        grids = []
        for f in range(6):
            blocks = []
            for i in range(2):
                k = 2 * j + i
                parts = [
                    spec[pl.ds(pl.multiple_of(((f * 2 + c) * levels + k) * full, full), full), :] for c in range(2)
                ]
                blocks.append(jnp.concatenate(parts, axis=0))
            block = jnp.concatenate(blocks, axis=1).astype(bf16)
            grids.append(jnp.dot(to_grid, block, preferred_element_type=f32))
        u, w = grids[:3], grids[3:]
        lamb = [
            u[1] * w[2] - u[2] * w[1],
            u[2] * w[0] - u[0] * w[2],
            u[0] * w[1] - u[1] * w[0],
        ]
        for f in range(3):
            made = jnp.dot(to_spec, lamb[f].astype(bf16), preferred_element_type=f32) * weight
            for i in range(2):
                k = 2 * j + i
                for c in range(2):
                    at = pl.multiple_of(((f * 2 + c) * levels + k) * full, full)
                    wgt[pl.ds(at, full), :] = made[c * full : (c + 1) * full, i * wide : (i + 1) * wide]
        return carry

    lax.fori_loop(0, levels // 2, middle, 0)

    def part_copy(d):
        return remote(part.at[d], part_in.at[d], part_send.at[d], part_recv.at[d], (origin(d), row))

    def analyse(d):
        heads = []
        tail = None
        for c in range(chunks):
            picked = []
            for p in range(c * per_chunk, (c + 1) * per_chunk):
                for i in range(2):
                    picked.append(wgt[pl.ds(d * slots + 2 * p + i, fields2, stride=full), :])
            lhs = jnp.concatenate(picked, axis=1).astype(bf16)
            first = c * per_chunk * 2 * wide
            made = jnp.dot(lhs, ops[d, first : first + per_chunk * 2 * wide, :], preferred_element_type=f32)
            heads.append(made[:, :wide])
            tail = made[:, wide:] if tail is None else tail + made[:, wide:]
        return jnp.concatenate(heads + [tail], axis=1)

    def project(i, carry):
        d = n_ma - i
        part[d] = analyse(d).astype(bf16)
        part_copy(d).start()
        return carry

    lax.fori_loop(1, n_ma, project, 0)
    source = analyse(0)

    def gather(i, total):
        d = n_ma - i
        part_copy(d).wait_recv()
        return total + part_in[d].astype(f32)

    source = lax.fori_loop(1, n_ma, gather, source)
    tail = source[:, main:]
    for shift in (8, 16, 32):
        tail = tail + pltpu.roll(tail, wide - shift, 1)
    own_tail = rest_t[0:fields2, :]
    heads = [source[:, c * wide : (c + 1) * wide] + coef_ref[c, 0:fields2].astype(f32) for c in range(chunks)]
    source = jnp.concatenate(heads + [tail + own_tail], axis=1)
    source = source.reshape(fields2 // levels, levels, lanes)
    own_levels = [source[:, k, :] for k in range(levels)]
    for i in range(2):
        halo[0, i] = own_levels[i].astype(bf16)
        halo[1, i] = own_levels[levels - 2 + i].astype(bf16)
    to_left = remote(halo.at[0], ext.at[1], halo_send.at[0], halo_recv.at[1], (me, left))
    to_right = remote(halo.at[1], ext.at[0], halo_send.at[1], halo_recv.at[0], (me, right))
    from_left = remote(halo.at[1], ext.at[0], halo_send.at[1], halo_recv.at[0], (me, left))
    from_right = remote(halo.at[0], ext.at[1], halo_send.at[0], halo_recv.at[1], (me, right))

    @pl.when(row > 0)
    def _():
        to_left.start()

    @pl.when(row < n_row - 1)
    def _():
        to_right.start()

    for s in range(1, n_ma):
        coef_copy(s).wait_send()
        leg_copy(s).wait_send()
        swap_copy(s).wait_send()
        rest_copy(s).wait_send()
        part_copy(s).wait_send()

    @pl.when(row > 0)
    def _():
        to_left.wait_send()
        from_left.wait_recv()

    @pl.when(row == 0)
    def _():
        ext[0] = jnp.zeros(ext.shape[1:], bf16)

    @pl.when(row < n_row - 1)
    def _():
        to_right.wait_send()
        from_right.wait_recv()

    @pl.when(row == n_row - 1)
    def _():
        ext[1] = jnp.zeros(ext.shape[1:], bf16)

    shape = (fields2 // levels, lanes)
    has_left = (row > 0).astype(f32)
    has_right = (row < n_row - 1).astype(f32)
    wide_levels = [ext[0, i].astype(f32) for i in range(2)] + own_levels + [ext[1, i].astype(f32) for i in range(2)]
    coupling = [jnp.full(shape, dif_ref[lax.rem((row + n_row) * levels + i - 2, n_row * levels)]) for i in range(levels + 4)]
    inverse = [1.0 / (1.0 + 2.0 * c) for c in coupling]
    first = [
        (wide_levels[i] + coupling[i] * (wide_levels[i - 1] + wide_levels[i + 1])) * inverse[i]
        for i in range(1, levels + 3)
    ]
    first[0] = first[0] * has_left
    first[-1] = first[-1] * has_right
    for k in range(levels):
        done = (wide_levels[k + 2] + coupling[k + 2] * (first[k] + first[k + 2])) * inverse[k + 2]
        for p in range(pairs):
            line = jnp.concatenate(
                [done[:, p * orders : (p + 1) * orders], done[:, main + p : main + p + 1]], axis=1
            )
            for i in range(fields2 // levels):
                out_ref[i * levels + k, p : p + 1, :] = line[i : i + 1]


def fused(velocity, vorticity, legendre, pair_order, lat_weight, diffusivity):
    n_ma = lax.axis_size("ma")
    n_row = lax.axis_size("row")
    pairs, rows, half_lat = legendre.shape
    levels = velocity.shape[2]
    orders = rows - 1
    main = pairs * orders
    chunks = main // 128
    lanes = main + 128
    lat = half_lat // n_ma
    slots = 2 * pairs
    full = n_ma * slots
    points = lon_count(orders)
    bf16 = jnp.bfloat16
    f32 = jnp.float32
    groups = 12 * levels
    scale = (NLON / points) / math.sqrt(NLON) / orders
    angle = np.outer(np.arange(orders), np.arange(points)) % points * (2.0 * math.pi / points)
    table = np.stack([np.cos(angle), -np.sin(angle)])
    tab = jnp.asarray(table, bf16)
    tab_t = jnp.asarray(np.transpose(table, (0, 2, 1)), bf16)
    vmem = pl.BlockSpec(memory_space=pltpu.VMEM)
    away = pl.BlockSpec(memory_space=pltpu.HBM)
    operands = (
        velocity.reshape(6 * levels, pairs, rows),
        vorticity.reshape(6 * levels, pairs, rows),
        jnp.transpose(legendre, (1, 0, 2)),
        pair_order,
        lat_weight,
        diffusivity,
        tab,
        tab_t,
    )
    out = pl.pallas_call(
        functools.partial(fused_kernel, n_ma, n_row, pairs, rows, levels, scale),
        out_shape=jax.ShapeDtypeStruct((6 * levels, pairs, rows), f32),
        in_specs=[away] * 8,
        out_specs=vmem,
        scratch_shapes=[
            pltpu.VMEM((6 * levels, pairs, rows), bf16),
            pltpu.VMEM((6 * levels, pairs, rows), bf16),
            pltpu.VMEM((rows, pairs, half_lat), bf16),
            pltpu.SMEM((pairs,), jnp.int32),
            pltpu.VMEM((half_lat,), f32),
            pltpu.SMEM(diffusivity.shape, f32),
            pltpu.VMEM(tab.shape, bf16),
            pltpu.VMEM(tab_t.shape, bf16),
            pltpu.SemaphoreType.DMA((8,)),
            pltpu.VMEM((half_lat // 128, rows * pairs + 4, 128), f32),
            pltpu.VMEM((n_ma, chunks, lat, 128), bf16),
            pltpu.VMEM((n_ma, 8, 128), bf16),
            pltpu.VMEM((n_ma, chunks, groups, 128), bf16),
            pltpu.VMEM((n_ma, chunks, lat, 128), bf16),
            pltpu.VMEM((n_ma, 8, 128), bf16),
            pltpu.VMEM((128, 128), f32),
            pltpu.VMEM((full, orders), f32),
            pltpu.VMEM((n_ma, pairs * 256, 256), bf16),
            pltpu.VMEM((groups * full, 128), f32),
            pltpu.VMEM((groups // 2 * full, 128), f32),
            pltpu.VMEM((n_ma, groups // 2, lanes), bf16),
            pltpu.VMEM((n_ma, groups // 2, lanes), bf16),
            pltpu.VMEM((2, 2, 6, lanes), bf16),
            pltpu.VMEM((2, 2, 6, lanes), bf16),
        ]
        + [pltpu.SemaphoreType.DMA((n_ma,))] * 10
        + [pltpu.SemaphoreType.DMA((2,))] * 2,
        compiler_params=pltpu.CompilerParams(
            collective_id=0, has_side_effects=True, vmem_limit_bytes=48 * 1024 * 1024
        ),
    )(*(pltpu.with_memory_space_constraint(x, pltpu.HBM) for x in operands))
    return out.reshape(velocity.shape)


def fits(velocity, legendre):
    n_ma = lax.axis_size("ma")
    n_row = lax.axis_size("row")
    pairs, rows, half_lat = legendre.shape
    levels = velocity.shape[2]
    lat = half_lat // n_ma
    tiles = pairs == 4 and pairs * (rows - 1) == 256 and n_ma % 2 == 0 and n_ma <= 8 and n_row % 2 == 0
    whole = half_lat % n_ma == 0 and half_lat % 128 == 0 and lat % 16 == 0 and lat <= 64 and levels == 4
    return tiles and whole and n_row > 2 and n_ma > 1


def step(velocity, vorticity, legendre, pair_order, lat_weight, diffusivity):
    chosen = fused if fits(velocity, legendre) else local
    return chosen(velocity, vorticity, legendre, pair_order, lat_weight, diffusivity)


def solution(mesh):
    in_specs = (
        P(None, None, "row", "ma", None),
        P(None, None, "row", "ma", None),
        P("ma", None, None),
        P("ma"),
        P(),
        P(),
    )
    out_specs = P(None, None, "row", "ma", None)
    return jax.shard_map(step, mesh=mesh, in_specs=in_specs, out_specs=out_specs, check_vma=False)
```

profile of v0, /device:TPU:1, one launch (start us, length us, event | category | flops | bytes accessed | tf_op | source)
XLA Modules:
  0.0 25.7 jit_solution(11122271067818317388)
XLA Ops:
  0.0 25.0 %shard_map.82 = f32[24,4,65]{2,1,0:T(4,128)S(1)} custom-call(bf16[24,4,65]{2,1,0:T(4,128)(2,1)} %bitcast.6, bf16[24,4,65]{2,1,0:T(4,128)(2,1)} %bitcast.7, bf16[65,4,384]{2,1,0:T(4,128)(2,1)} %bitcast.5, s32[4]{0:T(128)} %order_hbm.1, f32[384]{0:T(512)} %weight_hbm.1, f32[16]{0:T(128)} %dif_hbm.1, bf16[2,64,192]{2,1,0:T(8,128)(2,1)} %constant.4.clone.tab_hbm, ...), custom_call_target="tpu_custom_call" | custom-call | tf_op jit(solution)/shard_map/pallas_call | solution.py:558
  25.0 0.6 %copy.10 = f32[3,2,4,4,65]{4,3,2,1,0:T(4,128)} copy(f32[3,2,4,4,65]{4,3,2,1,0:T(4,128)S(1)} %bitcast.4) | data formatting | bytes 49920
where the time goes:
time: 25.8 us; the launch traced here: 25.7 us
  Pallas kernels  25 us (97%)
  local copies, waits for them, and re-layouts  0.62 us (2%)
    pallas_call x1, Pallas kernels, fused(): pl.pallas_call(functools.partial(fused_kernel, n_ma, n_row, pairs, rows,...  25 us
    unnamed x1, local copies, waits for them, and re-layouts  0.62 us

commit v1 on v0

--- a/solution.py
+++ b/solution.py
@@ -170,14 +170,13 @@
     velocity_hbm, vorticity_hbm, legendre_hbm, order_hbm, weight_hbm, dif_hbm, tab_hbm, tab_t_hbm,
     out_ref,
     velocity_ref, vorticity_ref, legendre_ref, order_ref, weight_ref, dif_ref, tab_ref, tab_t_ref, load_sem,
-    leg_rows, leg_ref, rest_ref, coef_all, leg_all, rest_all, rest_t, onehot, ops, spec, wgt, part, part_in, ext, halo,
-    coef_send, coef_recv, leg_send, leg_recv, swap_send, swap_recv, rest_send, rest_recv, part_send, part_recv, halo_send, halo_recv,
+    leg_rows, leg_ref, rest_ref, coef_all, leg_all, rest_all, rest_t, end_op, end_spec, onehot, ops, spec, wgt, part, part_in, far_in, far_sum, near_out, near_in,
+    coef_send, coef_recv, leg_send, leg_recv, swap_send, swap_recv, rest_send, rest_recv, part_send, part_recv, far_send, far_recv, near_send, near_recv, ready,
 ):
     me = lax.axis_index("ma")
     row = lax.axis_index("row")
     _, chunks, groups, wide = coef_all.shape
     coef_ref = coef_all.at[0]
-    lanes = (chunks + 1) * wide
     fields2 = groups // 2
     orders = rows - 1
     slots = 2 * pairs
@@ -190,6 +189,7 @@
     bf16 = jnp.bfloat16
     n_z = n_ma // 2
     z, y = me // 2, lax.rem(me, 2)
+    mate = me + 1 - 2 * y
     half = lax.rem(row, 2)
     mate_row = row + 1 - 2 * half
 
@@ -199,16 +199,19 @@
     def origin(s):
         return lax.rem(z + n_z - s // 2, n_z) * 2 + lax.rem(y + lax.rem(s, 2), 2)
 
-    left = lax.rem(row + n_row - 1, n_row)
-    right = lax.rem(row + 1, n_row)
+    far_row = row + 2 * half - 1
+    has_far = (far_row >= 0) & (far_row < n_row)
 
     barrier = pltpu.get_barrier_semaphore()
     for d in range(1, n_ma):
         pl.semaphore_signal(
             barrier, inc=1, device_id=(lax.rem(me + d, n_ma), row), device_id_type=pl.DeviceIdType.MESH
         )
-    for beside in (left, right):
-        pl.semaphore_signal(barrier, inc=1, device_id=(me, beside), device_id_type=pl.DeviceIdType.MESH)
+    pl.semaphore_signal(barrier, inc=1, device_id=(me, mate_row), device_id_type=pl.DeviceIdType.MESH)
+
+    @pl.when(has_far)
+    def _():
+        pl.semaphore_signal(barrier, inc=1, device_id=(me, far_row), device_id_type=pl.DeviceIdType.MESH)
 
     loads = [
         pltpu.make_async_copy(src, dst, load_sem.at[i])
@@ -265,39 +268,43 @@
         for b in range(n_ma):
             leg_ref[b, c] = turned[b * lat : (b + 1) * lat]
 
-    pl.semaphore_wait(barrier, n_ma + 1)
+    pl.semaphore_wait(barrier, n_ma + has_far.astype(jnp.int32))
+
+    relayed = n_ma // 2
 
     def coef_copy(s):
+        if s == relayed + 1:
+            return remote(coef_all.at[relayed], coef_all.at[s], coef_send.at[s], coef_recv.at[s], (mate, row))
         return remote(coef_ref, coef_all.at[s], coef_send.at[s], coef_recv.at[s], (target(s), row))
 
     def leg_copy(s):
         peer = target(s)
-        return remote(
-            leg_ref.at[peer, half], leg_all.at[s, half], leg_send.at[s], leg_recv.at[s], (peer, row)
-        )
-
-    def swap_copy(s):
-        return remote(
-            leg_all.at[s, half], leg_all.at[s, half], swap_send.at[s], swap_recv.at[s], (me, mate_row)
-        )
-
-    def swap_arrival(s):
-        return remote(
-            leg_all.at[s, half], leg_all.at[s, 1 - half], swap_send.at[s], swap_recv.at[s], (me, mate_row)
-        )
+        return remote(leg_ref.at[peer], leg_all.at[s], leg_send.at[s], leg_recv.at[s], (peer, row))
+
+    def share_copy(s):
+        return remote(leg_all.at[s], leg_all.at[s], swap_send.at[s], swap_recv.at[s], (me, mate_row))
 
     def rest_copy(s):
         peer = target(s)
         return remote(rest_ref.at[peer], rest_all.at[s], rest_send.at[s], rest_recv.at[s], (peer, row))
 
-    far_first = sorted(range(1, n_ma), key=lambda s: (-min(s // 2, n_z - s // 2), -(s % 2)))
-    near_first = far_first[::-1]
+    far_first = sorted(range(1, n_ma), key=lambda s: (-min(s // 2, n_z - s // 2), -(s // 2), s % 2))
+    direct = sorted((s for s in far_first if s // 2 * 2 != relayed), key=lambda s: (s < 2, -(s % 2), -s))
     for s in far_first:
         rest_copy(s).start()
-    for s in far_first:
-        leg_copy(s).start()
-    for s in far_first:
+    coef_copy(relayed).start()
+
+    @pl.when(half == 1)
+    def _():
+        for s in far_first:
+            leg_copy(s).start()
+
+    for s in direct:
         coef_copy(s).start()
+
+    @pl.when(has_far)
+    def _():
+        pl.semaphore_signal(ready, inc=1, device_id=(me, far_row), device_id_type=pl.DeviceIdType.MESH)
 
     leg_all[0] = leg_ref[me]
     rest_all[0] = rest_ref[me]
@@ -335,38 +342,56 @@
             order = jnp.where(m_sub == 2 * p + 1, orders - 1 - value, order)
         onehot[d * slots : (d + 1) * slots, :] = (m_lane == order).astype(f32)
 
-    def synth(d):
+    def build(d):
         low = low_orders(d)
         lower = lane_row < orders - low
         north_low = (own & lower).astype(f32)
         north_high = (own & jnp.logical_not(lower)).astype(f32)
         south_low = north_low * (1 - 2 * (lane_row & 1)).astype(f32)
         south_high = north_high * (1 - 2 * ((lane_row + low) & 1)).astype(f32)
-        north_end = (lane == 8 * d + sub).astype(f32)
-        south_end = north_end * (1 - 2 * (low & 1)).astype(f32)
-        end_leg = rest_t[side : side + lat, :]
-        end_coef = rest_t[0:groups, :].astype(bf16)
         for p in range(pairs):
             c = p // per_chunk
             table = leg_all[d, c].astype(f32)
             at = p * 2 * wide
             for i, factor in enumerate((north_low, south_low, north_high, south_high)):
-                ops[d, at + i * side : at + i * side + lat, 0:wide] = (table * factor[p : p + 1]).astype(bf16)
-            for i, factor in enumerate((north_end, south_end)):
-                first = at + wide + i * side
-                ops[d, first : first + lat, wide : 2 * wide] = (end_leg * factor[p : p + 1]).astype(bf16)
-            lhs = jnp.concatenate([coef_all[d, c], end_coef], axis=1)
+                ops[d, at + i * side : at + i * side + lat, :] = (table * factor[p : p + 1]).astype(bf16)
+
+    def synth(d):
+        for p in range(pairs):
+            at = p * 2 * wide
             made = lax.dot_general(
-                lhs, ops[d, at : at + 2 * wide, :], (((1,), (1,)), ((), ())), preferred_element_type=f32
+                coef_all[d, p // per_chunk],
+                ops[d, at : at + 2 * wide, :],
+                (((1,), (1,)), ((), ())),
+                preferred_element_type=f32,
             )
-            for i in range(2):
-                spec[pl.ds(d * slots + 2 * p + i, groups, stride=full), :] = made[:, i * wide : (i + 1) * wide]
-
-    for s in near_first:
+            spec[pl.ds(d * slots + 2 * p, groups, stride=full), :] = made[:, :wide]
+            spec[pl.ds(d * slots + 2 * p + 1, groups, stride=full), :] = made[:, wide:] + end_spec[d * pairs + p]
+
+    for s in far_first:
         rest_copy(s).wait_recv()
+    coef_copy(relayed).wait_recv()
+    coef_copy(relayed + 1).start()
+
+    def legs(ids):
+        @pl.when(half == 1)
+        def _():
+            for s in ids:
+                leg_copy(s).wait_recv()
+                share_copy(s).start()
+
+        @pl.when(half == 0)
+        def _():
+            for s in ids:
+                share_copy(s).wait_recv()
+
     rest = rest_all[...].astype(f32).reshape(n_ma * 8, wide)
-    rest = jnp.concatenate([rest, jnp.zeros((wide - n_ma * 8, wide), f32)], axis=0)
-    rest_t[...] = jnp.transpose(rest)
+    rest_t[...] = jnp.transpose(jnp.concatenate([rest, jnp.zeros((wide - n_ma * 8, wide), f32)], axis=0))
+    end_lane = lax.broadcasted_iota(jnp.int32, rest.shape, 1)
+    end_sign = (1 - 2 * (pltpu.roll(rest, n_ma * 8 - pairs, 0).astype(jnp.int32) & 1)).astype(f32)
+    north_end = jnp.where(end_lane < lat, pltpu.roll(rest, side, 1), 0.0)
+    south_end = jnp.where((end_lane >= side) & (end_lane < side + lat), rest * end_sign, 0.0)
+    end_op[...] = north_end + south_end
     for d in range(n_ma):
         place(d)
     hot = onehot[...].astype(bf16)
@@ -380,13 +405,36 @@
     to_spec = jnp.concatenate(
         [jnp.dot(hot, tab_ref[c], preferred_element_type=f32) for c in range(2)], axis=0
     ).astype(bf16)
+    for d in range(n_ma):
+        for p in range(pairs):
+            i = 8 * d + p
+            end_spec[d * pairs + p] = rest_t[0:groups, i : i + 1] * end_op[i : i + 1, :]
+    held = [coef_ref[c, 0:fields2].astype(f32) for c in range(chunks)]
+    held = jnp.concatenate(held + [rest_t[0:fields2, :]], axis=1)
+    held = held.reshape(6, levels, held.shape[1])
+    held = [held[:, k, :] for k in range(levels)]
+    block = 6 * levels // 2
+    lower = jnp.concatenate([held[k][:, c * wide : (c + 1) * wide] for c in range(chunks) for k in (0, 1)], axis=0)
+    upper = jnp.concatenate([held[k][:, c * wide : (c + 1) * wide] for c in range(chunks) for k in (2, 3)], axis=0)
+    own_end = jnp.concatenate([h[:, main:] for h in held] + [jnp.zeros((wide - fields2, wide), f32)], axis=0)
+    own_end = jnp.where(lax.broadcasted_iota(jnp.int32, own_end.shape, 1) < pairs, own_end, 0.0)
+    own_velocity = jnp.concatenate([lower, jnp.transpose(own_end)[0:8], upper], axis=0)
+    build(0)
     synth(0)
-    for s in near_first:
-        leg_copy(s).wait_recv()
-        swap_copy(s).start()
-    for s in near_first:
+    legs(far_first[:4])
+    for s in far_first[:4]:
+        build(s)
+    synth(relayed)
+    legs(far_first[4:])
+    for s in far_first[4:]:
+        build(s)
+    for s in direct[:2]:
         coef_copy(s).wait_recv()
-        swap_arrival(s).wait_recv()
+    for s in direct[:2]:
+        synth(s)
+    for s in direct[2:] + [relayed + 1]:
+        coef_copy(s).wait_recv()
+    for s in direct[2:] + [relayed + 1]:
         synth(s)
 
     def middle(j, carry):
@@ -412,7 +460,7 @@
             for i in range(2):
                 k = 2 * j + i
                 for c in range(2):
-                    at = pl.multiple_of(((f * 2 + c) * levels + k) * full, full)
+                    at = pl.multiple_of((k * 6 + f * 2 + c) * full, full)
                     wgt[pl.ds(at, full), :] = made[c * full : (c + 1) * full, i * wide : (i + 1) * wide]
         return carry
 
@@ -421,29 +469,67 @@
     def part_copy(d):
         return remote(part.at[d], part_in.at[d], part_send.at[d], part_recv.at[d], (origin(d), row))
 
+    def rows_of(slot):
+        return wgt[pl.ds(slot, fields2, stride=full), :]
+
     def analyse(d):
         heads = []
-        tail = None
         for c in range(chunks):
-            picked = []
-            for p in range(c * per_chunk, (c + 1) * per_chunk):
-                for i in range(2):
-                    picked.append(wgt[pl.ds(d * slots + 2 * p + i, fields2, stride=full), :])
+            picked = [rows_of(d * slots + i) for i in range(2 * c * per_chunk, 2 * (c + 1) * per_chunk)]
             lhs = jnp.concatenate(picked, axis=1).astype(bf16)
             first = c * per_chunk * 2 * wide
-            made = jnp.dot(lhs, ops[d, first : first + per_chunk * 2 * wide, :], preferred_element_type=f32)
-            heads.append(made[:, :wide])
-            tail = made[:, wide:] if tail is None else tail + made[:, wide:]
-        return jnp.concatenate(heads + [tail], axis=1)
+            heads.append(
+                jnp.dot(lhs, ops[d, first : first + per_chunk * 2 * wide, :], preferred_element_type=f32)
+            )
+        lower = jnp.concatenate([h[:block] for h in heads], axis=0)
+        upper = jnp.concatenate([h[block:] for h in heads], axis=0)
+        return lower, upper
+
+    highs = jnp.concatenate([rows_of(2 * i + 1).astype(bf16) for i in range(n_ma * pairs)], axis=0)
+    ends = lax.dot_general(
+        highs, end_op[...].astype(bf16), (((1,), (1,)), ((), ())), preferred_element_type=f32
+    )
+    end_column = lax.broadcasted_iota(jnp.int32, (fields2, n_ma * 8), 1)
+    end_sum = jnp.zeros((fields2, n_ma * 8), f32)
+    for i in range(n_ma * pairs):
+        at = i // pairs * 8 + i % pairs
+        end_sum = jnp.where(end_column == at, ends[i * fields2 : (i + 1) * fields2], end_sum)
+    end_sum = jnp.concatenate([end_sum, jnp.zeros((fields2, wide - n_ma * 8), f32)], axis=1)
+    end_sum = jnp.transpose(jnp.concatenate([end_sum, jnp.zeros((wide - fields2, wide), f32)], axis=0))
+    body = chunks * block
+    for d in range(n_ma):
+        part[d, body : body + 8] = end_sum[8 * d : 8 * (d + 1)].astype(bf16)
+
+    sent = pl.ds(pl.multiple_of(half * body, 8), body + 8)
+
+    def far_copy(d):
+        return remote(part.at[d, sent], far_in.at[d], far_send.at[d], far_recv.at[d], (origin(d), far_row))
+
+    @pl.when(has_far)
+    def _():
+        pl.semaphore_wait(ready, 1)
 
     def project(i, carry):
         d = n_ma - i
-        part[d] = analyse(d).astype(bf16)
+        lower, upper = analyse(d)
+        part[d, 0:body] = lower.astype(bf16)
+        part[d, body + 8 :] = upper.astype(bf16)
         part_copy(d).start()
+
+        @pl.when(has_far)
+        def _():
+            far_copy(d).start()
+
         return carry
 
     lax.fori_loop(1, n_ma, project, 0)
-    source = analyse(0)
+    lower, upper = analyse(0)
+    source = jnp.concatenate([lower, end_sum[0:8], upper], axis=0) + own_velocity
+    part[0] = source.astype(bf16)
+
+    @pl.when(has_far)
+    def _():
+        far_copy(0).start()
 
     def gather(i, total):
         d = n_ma - i
@@ -451,59 +537,66 @@
         return total + part_in[d].astype(f32)
 
     source = lax.fori_loop(1, n_ma, gather, source)
-    tail = source[:, main:]
-    for shift in (8, 16, 32):
-        tail = tail + pltpu.roll(tail, wide - shift, 1)
-    own_tail = rest_t[0:fields2, :]
-    heads = [source[:, c * wide : (c + 1) * wide] + coef_ref[c, 0:fields2].astype(f32) for c in range(chunks)]
-    source = jnp.concatenate(heads + [tail + own_tail], axis=1)
-    source = source.reshape(fields2 // levels, levels, lanes)
-    own_levels = [source[:, k, :] for k in range(levels)]
+
+    def end_rows(values):
+        turned = jnp.transpose(jnp.concatenate([values, jnp.zeros((wide - 8, wide), f32)], axis=0))[0:fields2]
+        return jnp.where(lax.broadcasted_iota(jnp.int32, turned.shape, 1) < pairs, turned, 0.0)
+
+    def level_pair(values, ends):
+        made = []
+        for k in range(2):
+            heads = [values[c * block + 6 * k : c * block + 6 * (k + 1)] for c in range(chunks)]
+            made.append(jnp.concatenate(heads + [ends[6 * k : 6 * (k + 1)]], axis=1))
+        return made
+
+    turned = end_rows(source[body : body + 8])
+    own_levels = level_pair(source[0:body], turned[0:block]) + level_pair(source[body + 8 :], turned[block:fields2])
     for i in range(2):
-        halo[0, i] = own_levels[i].astype(bf16)
-        halo[1, i] = own_levels[levels - 2 + i].astype(bf16)
-    to_left = remote(halo.at[0], ext.at[1], halo_send.at[0], halo_recv.at[1], (me, left))
-    to_right = remote(halo.at[1], ext.at[0], halo_send.at[1], halo_recv.at[0], (me, right))
-    from_left = remote(halo.at[1], ext.at[0], halo_send.at[1], halo_recv.at[0], (me, left))
-    from_right = remote(halo.at[0], ext.at[1], halo_send.at[0], halo_recv.at[1], (me, right))
-
-    @pl.when(row > 0)
-    def _():
-        to_left.start()
-
-    @pl.when(row < n_row - 1)
-    def _():
-        to_right.start()
+        near_out[i] = jnp.where(half == 0, own_levels[levels - 2 + i], own_levels[i]).astype(bf16)
+    near_copy = remote(near_out, near_in, near_send.at[0], near_recv.at[0], (me, mate_row))
+    near_copy.start()
+
+    @pl.when(has_far)
+    def _():
+        def collect(d, total):
+            far_copy(d).wait_recv()
+            return total + far_in[d].astype(f32)
+
+        far_sum[...] = lax.fori_loop(0, n_ma, collect, jnp.zeros(far_sum.shape, f32))
+
+    @pl.when(jnp.logical_not(has_far))
+    def _():
+        far_sum[...] = jnp.zeros(far_sum.shape, f32)
+
+    far_body = far_sum[pl.ds(pl.multiple_of((1 - half) * 8, 8), body), :]
+    turned = end_rows(far_sum[pl.ds(pl.multiple_of(half * body, 8), 8), :])
+    far_levels = level_pair(far_body, jnp.where(half == 0, turned[block:fields2], turned[0:block]))
 
     for s in range(1, n_ma):
         coef_copy(s).wait_send()
-        leg_copy(s).wait_send()
-        swap_copy(s).wait_send()
         rest_copy(s).wait_send()
         part_copy(s).wait_send()
 
-    @pl.when(row > 0)
-    def _():
-        to_left.wait_send()
-        from_left.wait_recv()
-
-    @pl.when(row == 0)
-    def _():
-        ext[0] = jnp.zeros(ext.shape[1:], bf16)
-
-    @pl.when(row < n_row - 1)
-    def _():
-        to_right.wait_send()
-        from_right.wait_recv()
-
-    @pl.when(row == n_row - 1)
-    def _():
-        ext[1] = jnp.zeros(ext.shape[1:], bf16)
-
-    shape = (fields2 // levels, lanes)
+    @pl.when(half == 1)
+    def _():
+        for s in range(1, n_ma):
+            leg_copy(s).wait_send()
+            share_copy(s).wait_send()
+
+    @pl.when(has_far)
+    def _():
+        for s in range(n_ma):
+            far_copy(s).wait_send()
+
+    near_copy.wait()
+
+    shape = own_levels[0].shape
     has_left = (row > 0).astype(f32)
     has_right = (row < n_row - 1).astype(f32)
-    wide_levels = [ext[0, i].astype(f32) for i in range(2)] + own_levels + [ext[1, i].astype(f32) for i in range(2)]
+    near_levels = [near_in[i].astype(f32) for i in range(2)]
+    before = [jnp.where(half == 0, a, b) for a, b in zip(far_levels, near_levels)]
+    after = [jnp.where(half == 0, b, a) for a, b in zip(far_levels, near_levels)]
+    wide_levels = before + own_levels + after
     coupling = [jnp.full(shape, dif_ref[lax.rem((row + n_row) * levels + i - 2, n_row * levels)]) for i in range(levels + 4)]
     inverse = [1.0 / (1.0 + 2.0 * c) for c in coupling]
     first = [
@@ -577,17 +670,22 @@
             pltpu.VMEM((n_ma, chunks, lat, 128), bf16),
             pltpu.VMEM((n_ma, 8, 128), bf16),
             pltpu.VMEM((128, 128), f32),
+            pltpu.VMEM((n_ma * 8, 128), f32),
+            pltpu.VMEM((n_ma * pairs, groups, 128), f32),
             pltpu.VMEM((full, orders), f32),
-            pltpu.VMEM((n_ma, pairs * 256, 256), bf16),
+            pltpu.VMEM((n_ma, pairs * 256, 128), bf16),
             pltpu.VMEM((groups * full, 128), f32),
             pltpu.VMEM((groups // 2 * full, 128), f32),
-            pltpu.VMEM((n_ma, groups // 2, lanes), bf16),
-            pltpu.VMEM((n_ma, groups // 2, lanes), bf16),
-            pltpu.VMEM((2, 2, 6, lanes), bf16),
-            pltpu.VMEM((2, 2, 6, lanes), bf16),
+            pltpu.VMEM((n_ma, chunks * groups // 2 + 8, 128), bf16),
+            pltpu.VMEM((n_ma, chunks * groups // 2 + 8, 128), bf16),
+            pltpu.VMEM((n_ma, chunks * groups // 4 + 8, 128), bf16),
+            pltpu.VMEM((chunks * groups // 4 + 8, 128), f32),
+            pltpu.VMEM((2, 6, lanes), bf16),
+            pltpu.VMEM((2, 6, lanes), bf16),
         ]
-        + [pltpu.SemaphoreType.DMA((n_ma,))] * 10
-        + [pltpu.SemaphoreType.DMA((2,))] * 2,
+        + [pltpu.SemaphoreType.DMA((n_ma,))] * 12
+        + [pltpu.SemaphoreType.DMA((1,))] * 2
+        + [pltpu.SemaphoreType.REGULAR],
         compiler_params=pltpu.CompilerParams(
             collective_id=0, has_side_effects=True, vmem_limit_bytes=48 * 1024 * 1024
         ),

time: 25.8 us -> 23.4 us (0.907)
  Pallas kernels: 25 us -> 22.5 us
    pallas_call x1, Pallas kernels: 25 us -> 22.5 us  [fused(): pl.pallas_call(functools.partial(fused_kernel, n_ma, n_row, pairs, rows,...]
where the time goes in v1:
time: 23.4 us; the launch traced here: 23.1 us
  Pallas kernels  22.5 us (96%)
  local copies, waits for them, and re-layouts  0.62 us (3%)
    pallas_call x1, Pallas kernels, fused(): pl.pallas_call(functools.partial(fused_kernel, n_ma, n_row, pairs, rows,...  22.5 us
    unnamed x1, local copies, waits for them, and re-layouts  0.62 us

profile of v1, /device:TPU:1, one launch (start us, length us, event | category | flops | bytes accessed | tf_op | source)
XLA Modules:
  0.0 23.1 jit_solution(6362233365143074694)
XLA Ops:
  0.0 22.5 %shard_map.82 = f32[24,4,65]{2,1,0:T(4,128)S(1)} custom-call(bf16[24,4,65]{2,1,0:T(4,128)(2,1)} %bitcast.6, bf16[24,4,65]{2,1,0:T(4,128)(2,1)} %bitcast.7, bf16[65,4,384]{2,1,0:T(4,128)(2,1)} %bitcast.5, s32[4]{0:T(128)} %order_hbm.1, f32[384]{0:T(512)} %weight_hbm.1, f32[16]{0:T(128)} %dif_hbm.1, bf16[2,64,192]{2,1,0:T(8,128)(2,1)} %constant.4.clone.tab_hbm, ...), custom_call_target="tpu_custom_call" | custom-call | tf_op jit(solution)/shard_map/pallas_call | solution.py:651
  22.5 0.6 %copy.10 = f32[3,2,4,4,65]{4,3,2,1,0:T(4,128)} copy(f32[3,2,4,4,65]{4,3,2,1,0:T(4,128)S(1)} %bitcast.4) | data formatting | bytes 49920

commit v2 on v1

--- a/solution.py
+++ b/solution.py
@@ -270,29 +270,39 @@
 
     pl.semaphore_wait(barrier, n_ma + has_far.astype(jnp.int32))
 
-    relayed = n_ma // 2
+    passed = [s for s in (4,) if s < n_ma]
+    gained = [s + 1 for s in passed]
+    far_first = sorted(range(1, n_ma), key=lambda s: (-min(s // 2, n_z - s // 2), -(s // 2), s % 2))
+    direct = [s for s in (7, 3, 6, 2, 1) if s < n_ma]
+    coef_groups = [[s] for s in passed] + [direct[:2], direct[2:], gained]
+    leg_groups = [far_first[: n_ma // 2], far_first[n_ma // 2 :]]
+
+    def wait_blocks(ref, count, sem):
+        blocks = ref.at[pl.ds(0, count)]
+        pltpu.make_async_copy(blocks, blocks, sem).wait()
 
     def coef_copy(s):
-        if s == relayed + 1:
-            return remote(coef_all.at[relayed], coef_all.at[s], coef_send.at[s], coef_recv.at[s], (mate, row))
-        return remote(coef_ref, coef_all.at[s], coef_send.at[s], coef_recv.at[s], (target(s), row))
+        group = [s in g for g in coef_groups].index(True)
+        if s in gained:
+            return remote(coef_all.at[s - 1], coef_all.at[s], coef_send.at[0], coef_recv.at[group], (mate, row))
+        return remote(coef_ref, coef_all.at[s], coef_send.at[0], coef_recv.at[group], (target(s), row))
 
     def leg_copy(s):
         peer = target(s)
-        return remote(leg_ref.at[peer], leg_all.at[s], leg_send.at[s], leg_recv.at[s], (peer, row))
+        return remote(leg_ref.at[peer], leg_all.at[s], leg_send.at[0], leg_recv.at[s - 1], (peer, row))
 
     def share_copy(s):
-        return remote(leg_all.at[s], leg_all.at[s], swap_send.at[s], swap_recv.at[s], (me, mate_row))
+        group = [s in g for g in leg_groups].index(True)
+        return remote(leg_all.at[s], leg_all.at[s], swap_send.at[0], swap_recv.at[group], (me, mate_row))
 
     def rest_copy(s):
         peer = target(s)
-        return remote(rest_ref.at[peer], rest_all.at[s], rest_send.at[s], rest_recv.at[s], (peer, row))
-
-    far_first = sorted(range(1, n_ma), key=lambda s: (-min(s // 2, n_z - s // 2), -(s // 2), s % 2))
-    direct = sorted((s for s in far_first if s // 2 * 2 != relayed), key=lambda s: (s < 2, -(s % 2), -s))
+        return remote(rest_ref.at[peer], rest_all.at[s], rest_send.at[0], rest_recv.at[0], (peer, row))
+
     for s in far_first:
         rest_copy(s).start()
-    coef_copy(relayed).start()
+    for s in passed:
+        coef_copy(s).start()
 
     @pl.when(half == 1)
     def _():
@@ -368,22 +378,21 @@
             spec[pl.ds(d * slots + 2 * p, groups, stride=full), :] = made[:, :wide]
             spec[pl.ds(d * slots + 2 * p + 1, groups, stride=full), :] = made[:, wide:] + end_spec[d * pairs + p]
 
-    for s in far_first:
-        rest_copy(s).wait_recv()
-    coef_copy(relayed).wait_recv()
-    coef_copy(relayed + 1).start()
-
-    def legs(ids):
+    for i, s in enumerate(passed):
+        wait_blocks(coef_all, 1, coef_recv.at[i])
+        coef_copy(s + 1).start()
+    wait_blocks(rest_all, n_ma - 1, rest_recv.at[0])
+
+    def legs(group):
         @pl.when(half == 1)
         def _():
-            for s in ids:
+            for s in leg_groups[group]:
                 leg_copy(s).wait_recv()
                 share_copy(s).start()
 
         @pl.when(half == 0)
         def _():
-            for s in ids:
-                share_copy(s).wait_recv()
+            wait_blocks(leg_all, len(leg_groups[group]), swap_recv.at[group])
 
     rest = rest_all[...].astype(f32).reshape(n_ma * 8, wide)
     rest_t[...] = jnp.transpose(jnp.concatenate([rest, jnp.zeros((wide - n_ma * 8, wide), f32)], axis=0))
@@ -421,21 +430,18 @@
     own_velocity = jnp.concatenate([lower, jnp.transpose(own_end)[0:8], upper], axis=0)
     build(0)
     synth(0)
-    legs(far_first[:4])
-    for s in far_first[:4]:
+    legs(0)
+    for s in leg_groups[0]:
         build(s)
-    synth(relayed)
-    legs(far_first[4:])
-    for s in far_first[4:]:
+    for s in passed:
+        synth(s)
+    legs(1)
+    for s in leg_groups[1]:
         build(s)
-    for s in direct[:2]:
-        coef_copy(s).wait_recv()
-    for s in direct[:2]:
-        synth(s)
-    for s in direct[2:] + [relayed + 1]:
-        coef_copy(s).wait_recv()
-    for s in direct[2:] + [relayed + 1]:
-        synth(s)
+    for group in range(len(passed), len(coef_groups)):
+        wait_blocks(coef_all, len(coef_groups[group]), coef_recv.at[group])
+        for s in coef_groups[group]:
+            synth(s)
 
     def middle(j, carry):
         grids = []
@@ -467,7 +473,7 @@
     lax.fori_loop(0, levels // 2, middle, 0)
 
     def part_copy(d):
-        return remote(part.at[d], part_in.at[d], part_send.at[d], part_recv.at[d], (origin(d), row))
+        return remote(part.at[d], part_in.at[d], part_send.at[0], part_recv.at[0], (origin(d), row))
 
     def rows_of(slot):
         return wgt[pl.ds(slot, fields2, stride=full), :]
@@ -485,7 +491,7 @@
         upper = jnp.concatenate([h[block:] for h in heads], axis=0)
         return lower, upper
 
-    highs = jnp.concatenate([rows_of(2 * i + 1).astype(bf16) for i in range(n_ma * pairs)], axis=0)
+    highs = jnp.concatenate([rows_of(2 * i + 1) for i in range(n_ma * pairs)], axis=0).astype(bf16)
     ends = lax.dot_general(
         highs, end_op[...].astype(bf16), (((1,), (1,)), ((), ())), preferred_element_type=f32
     )
@@ -503,14 +509,16 @@
     sent = pl.ds(pl.multiple_of(half * body, 8), body + 8)
 
     def far_copy(d):
-        return remote(part.at[d, sent], far_in.at[d], far_send.at[d], far_recv.at[d], (origin(d), far_row))
+        return remote(part.at[d, sent], far_in.at[d], far_send.at[0], far_recv.at[0], (origin(d), far_row))
 
     @pl.when(has_far)
     def _():
         pl.semaphore_wait(ready, 1)
 
+    upper_z = z // (n_z // 2)
+
     def project(i, carry):
-        d = n_ma - i
+        d = upper_z * (n_ma - i) + (1 - upper_z) * (1 + lax.rem(i, n_ma - 1))
         lower, upper = analyse(d)
         part[d, 0:body] = lower.astype(bf16)
         part[d, body + 8 :] = upper.astype(bf16)
@@ -531,12 +539,9 @@
     def _():
         far_copy(0).start()
 
-    def gather(i, total):
-        d = n_ma - i
-        part_copy(d).wait_recv()
-        return total + part_in[d].astype(f32)
-
-    source = lax.fori_loop(1, n_ma, gather, source)
+    wait_blocks(part_in, n_ma - 1, part_recv.at[0])
+    for d in range(1, n_ma):
+        source = source + part_in[d].astype(f32)
 
     def end_rows(values):
         turned = jnp.transpose(jnp.concatenate([values, jnp.zeros((wide - 8, wide), f32)], axis=0))[0:fields2]
@@ -558,11 +563,11 @@
 
     @pl.when(has_far)
     def _():
-        def collect(d, total):
-            far_copy(d).wait_recv()
-            return total + far_in[d].astype(f32)
-
-        far_sum[...] = lax.fori_loop(0, n_ma, collect, jnp.zeros(far_sum.shape, f32))
+        wait_blocks(far_in, n_ma, far_recv.at[0])
+        total = far_in[0].astype(f32)
+        for d in range(1, n_ma):
+            total = total + far_in[d].astype(f32)
+        far_sum[...] = total
 
     @pl.when(jnp.logical_not(has_far))
     def _():
@@ -572,21 +577,18 @@
     turned = end_rows(far_sum[pl.ds(pl.multiple_of(half * body, 8), 8), :])
     far_levels = level_pair(far_body, jnp.where(half == 0, turned[block:fields2], turned[0:block]))
 
-    for s in range(1, n_ma):
-        coef_copy(s).wait_send()
-        rest_copy(s).wait_send()
-        part_copy(s).wait_send()
+    wait_blocks(coef_all, n_ma - 1, coef_send.at[0])
+    wait_blocks(rest_all, n_ma - 1, rest_send.at[0])
+    wait_blocks(part_in, n_ma - 1, part_send.at[0])
 
     @pl.when(half == 1)
     def _():
-        for s in range(1, n_ma):
-            leg_copy(s).wait_send()
-            share_copy(s).wait_send()
+        wait_blocks(leg_all, n_ma - 1, leg_send.at[0])
+        wait_blocks(leg_all, n_ma - 1, swap_send.at[0])
 
     @pl.when(has_far)
     def _():
-        for s in range(n_ma):
-            far_copy(s).wait_send()
+        wait_blocks(far_in, n_ma, far_send.at[0])
 
     near_copy.wait()
 
@@ -683,8 +685,7 @@
             pltpu.VMEM((2, 6, lanes), bf16),
             pltpu.VMEM((2, 6, lanes), bf16),
         ]
-        + [pltpu.SemaphoreType.DMA((n_ma,))] * 12
-        + [pltpu.SemaphoreType.DMA((1,))] * 2
+        + [pltpu.SemaphoreType.DMA((count,)) for count in (1, 6, 1, n_ma - 1, 1, 2, 1, 1, 1, 1, 1, 1, 1, 1)]
         + [pltpu.SemaphoreType.REGULAR],
         compiler_params=pltpu.CompilerParams(
             collective_id=0, has_side_effects=True, vmem_limit_bytes=48 * 1024 * 1024

time: 23.4 us -> 22.3 us (0.953)
  Pallas kernels: 22.5 us -> 21.4 us
    pallas_call x1, Pallas kernels: 22.5 us -> 21.4 us  [fused(): pl.pallas_call(functools.partial(fused_kernel, n_ma, n_row, pairs, rows,...]
where the time goes in v2:
time: 22.3 us; the launch traced here: 22 us
  Pallas kernels  21.4 us (96%)
  local copies, waits for them, and re-layouts  0.62 us (3%)
    pallas_call x1, Pallas kernels, fused(): pl.pallas_call(functools.partial(fused_kernel, n_ma, n_row, pairs, rows,...  21.4 us
    unnamed x1, local copies, waits for them, and re-layouts  0.62 us

profile of v2, /device:TPU:1, one launch (start us, length us, event | category | flops | bytes accessed | tf_op | source)
XLA Modules:
  0.0 22.0 jit_solution(9396000938893721758)
XLA Ops:
  0.0 21.4 %shard_map.82 = f32[24,4,65]{2,1,0:T(4,128)S(1)} custom-call(bf16[24,4,65]{2,1,0:T(4,128)(2,1)} %bitcast.6, bf16[24,4,65]{2,1,0:T(4,128)(2,1)} %bitcast.7, bf16[65,4,384]{2,1,0:T(4,128)(2,1)} %bitcast.5, s32[4]{0:T(128)} %order_hbm.1, f32[384]{0:T(512)} %weight_hbm.1, f32[16]{0:T(128)} %dif_hbm.1, bf16[2,64,192]{2,1,0:T(8,128)(2,1)} %constant.4.clone.tab_hbm, ...), custom_call_target="tpu_custom_call" | custom-call | tf_op jit(solution)/shard_map/pallas_call | solution.py:653
  21.4 0.6 %copy.10 = f32[3,2,4,4,65]{4,3,2,1,0:T(4,128)} copy(f32[3,2,4,4,65]{4,3,2,1,0:T(4,128)S(1)} %bitcast.4) | data formatting | bytes 49920

commit v3 on v2

--- a/solution.py
+++ b/solution.py
@@ -443,14 +443,14 @@
         for s in coef_groups[group]:
             synth(s)
 
-    def middle(j, carry):
+    def middle(j):
         grids = []
         for f in range(6):
             blocks = []
             for i in range(2):
                 k = 2 * j + i
                 parts = [
-                    spec[pl.ds(pl.multiple_of(((f * 2 + c) * levels + k) * full, full), full), :] for c in range(2)
+                    spec[pl.ds(((f * 2 + c) * levels + k) * full, full), :] for c in range(2)
                 ]
                 blocks.append(jnp.concatenate(parts, axis=0))
             block = jnp.concatenate(blocks, axis=1).astype(bf16)
@@ -466,11 +466,11 @@
             for i in range(2):
                 k = 2 * j + i
                 for c in range(2):
-                    at = pl.multiple_of((k * 6 + f * 2 + c) * full, full)
+                    at = (k * 6 + f * 2 + c) * full
                     wgt[pl.ds(at, full), :] = made[c * full : (c + 1) * full, i * wide : (i + 1) * wide]
-        return carry
-
-    lax.fori_loop(0, levels // 2, middle, 0)
+
+    for j in range(levels // 2):
+        middle(j)
 
     def part_copy(d):
         return remote(part.at[d], part_in.at[d], part_send.at[0], part_recv.at[0], (origin(d), row))
@@ -491,6 +491,38 @@
         upper = jnp.concatenate([h[block:] for h in heads], axis=0)
         return lower, upper
 
+    body = chunks * block
+    sent = pl.ds(pl.multiple_of(half * body, 8), body + 8)
+
+    def far_copy(d):
+        return remote(part.at[d, sent], far_in.at[d], far_send.at[0], far_recv.at[0], (origin(d), far_row))
+
+    @pl.when(has_far)
+    def _():
+        pl.semaphore_wait(ready, 1)
+
+    upper_z = z // (n_z // 2)
+
+    def project(steps):
+        made = []
+        for i in steps:
+            d = upper_z * (n_ma - i) + (1 - upper_z) * (1 + lax.rem(i, n_ma - 1))
+            made.append((d, analyse(d)))
+        return made
+
+    def send(made):
+        for d, (lower, upper) in made:
+            part[d, 0:body] = lower.astype(bf16)
+            part[d, body + 8 :] = upper.astype(bf16)
+        for d, _ in made:
+            part_copy(d).start()
+
+        @pl.when(has_far)
+        def _():
+            for d, _ in made:
+                far_copy(d).start()
+
+    made = project([1, 2])
     highs = jnp.concatenate([rows_of(2 * i + 1) for i in range(n_ma * pairs)], axis=0).astype(bf16)
     ends = lax.dot_general(
         highs, end_op[...].astype(bf16), (((1,), (1,)), ((), ())), preferred_element_type=f32
@@ -502,36 +534,15 @@
         end_sum = jnp.where(end_column == at, ends[i * fields2 : (i + 1) * fields2], end_sum)
     end_sum = jnp.concatenate([end_sum, jnp.zeros((fields2, wide - n_ma * 8), f32)], axis=1)
     end_sum = jnp.transpose(jnp.concatenate([end_sum, jnp.zeros((wide - fields2, wide), f32)], axis=0))
-    body = chunks * block
     for d in range(n_ma):
         part[d, body : body + 8] = end_sum[8 * d : 8 * (d + 1)].astype(bf16)
 
-    sent = pl.ds(pl.multiple_of(half * body, 8), body + 8)
-
-    def far_copy(d):
-        return remote(part.at[d, sent], far_in.at[d], far_send.at[0], far_recv.at[0], (origin(d), far_row))
-
-    @pl.when(has_far)
-    def _():
-        pl.semaphore_wait(ready, 1)
-
-    upper_z = z // (n_z // 2)
-
-    def project(i, carry):
-        d = upper_z * (n_ma - i) + (1 - upper_z) * (1 + lax.rem(i, n_ma - 1))
-        lower, upper = analyse(d)
-        part[d, 0:body] = lower.astype(bf16)
-        part[d, body + 8 :] = upper.astype(bf16)
-        part_copy(d).start()
-
-        @pl.when(has_far)
-        def _():
-            far_copy(d).start()
-
-        return carry
-
-    lax.fori_loop(1, n_ma, project, 0)
+    send(made)
+    for i in range(3, n_ma - 1, 2):
+        send(project([i, i + 1]))
+    made = project([n_ma - 1])
     lower, upper = analyse(0)
+    send(made)
     source = jnp.concatenate([lower, end_sum[0:8], upper], axis=0) + own_velocity
     part[0] = source.astype(bf16)
 
@@ -590,7 +601,7 @@
     def _():
         wait_blocks(far_in, n_ma, far_send.at[0])
 
-    near_copy.wait()
+    near_copy.wait_recv()
 
     shape = own_levels[0].shape
     has_left = (row > 0).astype(f32)
@@ -615,6 +626,7 @@
             )
             for i in range(fields2 // levels):
                 out_ref[i * levels + k, p : p + 1, :] = line[i : i + 1]
+    near_copy.wait_send()
 
 
 def fused(velocity, vorticity, legendre, pair_order, lat_weight, diffusivity):

time: 22.3 us -> 21.9 us (0.982)
  Pallas kernels: 21.4 us -> 21.1 us
    pallas_call x1, Pallas kernels: 21.4 us -> 21.1 us  [fused(): pl.pallas_call(functools.partial(fused_kernel, n_ma, n_row, pairs, rows,...]
where the time goes in v3:
time: 21.9 us; the launch traced here: 21.8 us
  Pallas kernels  21.1 us (96%)
  local copies, waits for them, and re-layouts  0.62 us (3%)
    pallas_call x1, Pallas kernels, fused(): pl.pallas_call(functools.partial(fused_kernel, n_ma, n_row, pairs, rows,...  21.1 us
    unnamed x1, local copies, waits for them, and re-layouts  0.62 us

profile of v3, /device:TPU:1, one launch (start us, length us, event | category | flops | bytes accessed | tf_op | source)
XLA Modules:
  0.0 21.8 jit_solution(17463831626617437035)
XLA Ops:
  0.0 21.1 %shard_map.82 = f32[24,4,65]{2,1,0:T(4,128)S(1)} custom-call(bf16[24,4,65]{2,1,0:T(4,128)(2,1)} %bitcast.6, bf16[24,4,65]{2,1,0:T(4,128)(2,1)} %bitcast.7, bf16[65,4,384]{2,1,0:T(4,128)(2,1)} %bitcast.5, s32[4]{0:T(128)} %order_hbm.1, f32[384]{0:T(512)} %weight_hbm.1, f32[16]{0:T(128)} %dif_hbm.1, bf16[2,64,192]{2,1,0:T(8,128)(2,1)} %constant.4.clone.tab_hbm, ...), custom_call_target="tpu_custom_call" | custom-call | tf_op jit(solution)/shard_map/pallas_call | solution.py:665
  21.1 0.6 %copy.10 = f32[3,2,4,4,65]{4,3,2,1,0:T(4,128)} copy(f32[3,2,4,4,65]{4,3,2,1,0:T(4,128)S(1)} %bitcast.4) | data formatting | bytes 49920

commit v4 on v3

--- a/solution.py
+++ b/solution.py
@@ -248,11 +248,11 @@
     ends = jnp.concatenate([ends, jnp.zeros((wide - groups, wide), f32)], axis=0)
     ends = jnp.transpose(ends)[0:pairs, 0:side]
     tails = jnp.concatenate([leg_rows[t, main : main + pairs, :] for t in range(leg_rows.shape[0])], axis=1)
-    order_rows = [jnp.full((1, wide), order_ref[p].astype(f32)) for p in range(pairs)]
-    filler = jnp.zeros((pairs, side - lat), f32)
+    order_rows = [jnp.full((1, side - lat), order_ref[p].astype(f32)) for p in range(pairs)]
+    filler = jnp.concatenate(order_rows, axis=0)
     for b in range(n_ma):
         data_rows = jnp.concatenate([ends, tails[:, b * lat : (b + 1) * lat], filler], axis=1)
-        rest_ref[b] = jnp.concatenate([data_rows] + order_rows, axis=0).astype(bf16)
+        rest_ref[b] = data_rows.astype(bf16)
     for c in range(chunks):
         members = range(c * per_chunk, (c + 1) * per_chunk)
         coef_all[0, c] = jnp.concatenate([packs[p][:, :orders] for p in members], axis=1).astype(bf16)
@@ -341,7 +341,8 @@
     own = lane // orders == sub % per_chunk
 
     def low_orders(d):
-        return rest_all[d].astype(f32)[pairs:].astype(jnp.int32)
+        held_order = rest_all[d].astype(f32)[:, side + lat : side + lat + 1]
+        return jnp.broadcast_to(held_order, (pairs, wide)).astype(jnp.int32)
 
     def place(d):
         low = low_orders(d)
@@ -394,7 +395,10 @@
         def _():
             wait_blocks(leg_all, len(leg_groups[group]), swap_recv.at[group])
 
-    rest = rest_all[...].astype(f32).reshape(n_ma * 8, wide)
+    rest = []
+    for d in range(n_ma):
+        rest += [rest_all[d].astype(f32), low_orders(d).astype(f32)]
+    rest = jnp.concatenate(rest, axis=0)
     rest_t[...] = jnp.transpose(jnp.concatenate([rest, jnp.zeros((wide - n_ma * 8, wide), f32)], axis=0))
     end_lane = lax.broadcasted_iota(jnp.int32, rest.shape, 1)
     end_sign = (1 - 2 * (pltpu.roll(rest, n_ma * 8 - pairs, 0).astype(jnp.int32) & 1)).astype(f32)
@@ -514,13 +518,13 @@
         for d, (lower, upper) in made:
             part[d, 0:body] = lower.astype(bf16)
             part[d, body + 8 :] = upper.astype(bf16)
-        for d, _ in made:
-            part_copy(d).start()
-
         @pl.when(has_far)
         def _():
             for d, _ in made:
                 far_copy(d).start()
+
+        for d, _ in made:
+            part_copy(d).start()
 
     made = project([1, 2])
     highs = jnp.concatenate([rows_of(2 * i + 1) for i in range(n_ma * pairs)], axis=0).astype(bf16)
@@ -679,10 +683,10 @@
             pltpu.SemaphoreType.DMA((8,)),
             pltpu.VMEM((half_lat // 128, rows * pairs + 4, 128), f32),
             pltpu.VMEM((n_ma, chunks, lat, 128), bf16),
-            pltpu.VMEM((n_ma, 8, 128), bf16),
+            pltpu.VMEM((n_ma, pairs, 128), bf16),
             pltpu.VMEM((n_ma, chunks, groups, 128), bf16),
             pltpu.VMEM((n_ma, chunks, lat, 128), bf16),
-            pltpu.VMEM((n_ma, 8, 128), bf16),
+            pltpu.VMEM((n_ma, pairs, 128), bf16),
             pltpu.VMEM((128, 128), f32),
             pltpu.VMEM((n_ma * 8, 128), f32),
             pltpu.VMEM((n_ma * pairs, groups, 128), f32),
@@ -697,7 +701,7 @@
             pltpu.VMEM((2, 6, lanes), bf16),
             pltpu.VMEM((2, 6, lanes), bf16),
         ]
-        + [pltpu.SemaphoreType.DMA((count,)) for count in (1, 6, 1, n_ma - 1, 1, 2, 1, 1, 1, 1, 1, 1, 1, 1)]
+        + [pltpu.SemaphoreType.DMA((count,)) for count in (1, 4, 1, n_ma - 1, 1, 2, 1, 1, 1, 1, 1, 1, 1, 1)]
         + [pltpu.SemaphoreType.REGULAR],
         compiler_params=pltpu.CompilerParams(
             collective_id=0, has_side_effects=True, vmem_limit_bytes=48 * 1024 * 1024
@@ -712,8 +716,8 @@
     pairs, rows, half_lat = legendre.shape
     levels = velocity.shape[2]
     lat = half_lat // n_ma
-    tiles = pairs == 4 and pairs * (rows - 1) == 256 and n_ma % 2 == 0 and n_ma <= 8 and n_row % 2 == 0
-    whole = half_lat % n_ma == 0 and half_lat % 128 == 0 and lat % 16 == 0 and lat <= 64 and levels == 4
+    tiles = pairs == 4 and pairs * (rows - 1) == 256 and n_ma == 8 and n_row % 2 == 0
+    whole = half_lat % n_ma == 0 and half_lat % 128 == 0 and lat % 16 == 0 and lat < 64 and levels == 4
     return tiles and whole and n_row > 2 and n_ma > 1
 
 

time: 21.9 us -> 21.7 us (level)
  no operation moved by 1% of the time
where the time goes in v4:
time: 21.7 us; the launch traced here: 21.5 us
  Pallas kernels  20.9 us (96%)
  local copies, waits for them, and re-layouts  0.62 us (3%)
    pallas_call x1, Pallas kernels, fused(): pl.pallas_call(functools.partial(fused_kernel, n_ma, n_row, pairs, rows,...  20.9 us
    unnamed x1, local copies, waits for them, and re-layouts  0.62 us

profile of v4, /device:TPU:1, one launch (start us, length us, event | category | flops | bytes accessed | tf_op | source)
XLA Modules:
  0.0 21.5 jit_solution(14917839837344169943)
XLA Ops:
  0.0 20.9 %shard_map.82 = f32[24,4,65]{2,1,0:T(4,128)S(1)} custom-call(bf16[24,4,65]{2,1,0:T(4,128)(2,1)} %bitcast.6, bf16[24,4,65]{2,1,0:T(4,128)(2,1)} %bitcast.7, bf16[65,4,384]{2,1,0:T(4,128)(2,1)} %bitcast.5, s32[4]{0:T(128)} %order_hbm.1, f32[384]{0:T(512)} %weight_hbm.1, f32[16]{0:T(128)} %dif_hbm.1, bf16[2,64,192]{2,1,0:T(8,128)(2,1)} %constant.4.clone.tab_hbm, ...), custom_call_target="tpu_custom_call" | custom-call | tf_op jit(solution)/shard_map/pallas_call | solution.py:669
  20.9 0.6 %copy.10 = f32[3,2,4,4,65]{4,3,2,1,0:T(4,128)} copy(f32[3,2,4,4,65]{4,3,2,1,0:T(4,128)S(1)} %bitcast.4) | data formatting | bytes 49920

commit v5 on v4

--- a/solution.py
+++ b/solution.py
@@ -190,6 +190,7 @@
     n_z = n_ma // 2
     z, y = me // 2, lax.rem(me, 2)
     mate = me + 1 - 2 * y
+    upper_z = z // (n_z // 2)
     half = lax.rem(row, 2)
     mate_row = row + 1 - 2 * half
 
@@ -306,8 +307,11 @@
 
     @pl.when(half == 1)
     def _():
-        for s in far_first:
-            leg_copy(s).start()
+        for j in range(n_z - 1):
+            delta = upper_z * (1 + j) + (1 - upper_z) * (n_z - 1 - j)
+            leg_copy(2 * delta).start()
+            leg_copy(2 * delta + 1).start()
+        leg_copy(1).start()
 
     for s in direct:
         coef_copy(s).start()
@@ -505,8 +509,6 @@
     def _():
         pl.semaphore_wait(ready, 1)
 
-    upper_z = z // (n_z // 2)
-
     def project(steps):
         made = []
         for i in steps:

time: 21.7 us -> 21.7 us (level)
  no operation moved by 1% of the time
where the time goes in v5:
time: 21.7 us; the launch traced here: 21.5 us
  Pallas kernels  20.9 us (96%)
  local copies, waits for them, and re-layouts  0.62 us (3%)
    pallas_call x1, Pallas kernels, fused(): pl.pallas_call(functools.partial(fused_kernel, n_ma, n_row, pairs, rows,...  20.9 us
    unnamed x1, local copies, waits for them, and re-layouts  0.62 us

profile of v5, /device:TPU:1, one launch (start us, length us, event | category | flops | bytes accessed | tf_op | source)
XLA Modules:
  0.0 21.5 jit_solution(14780632218172539309)
XLA Ops:
  0.0 20.9 %shard_map.82 = f32[24,4,65]{2,1,0:T(4,128)S(1)} custom-call(bf16[24,4,65]{2,1,0:T(4,128)(2,1)} %bitcast.6, bf16[24,4,65]{2,1,0:T(4,128)(2,1)} %bitcast.7, bf16[65,4,384]{2,1,0:T(4,128)(2,1)} %bitcast.5, s32[4]{0:T(128)} %order_hbm.1, f32[384]{0:T(512)} %weight_hbm.1, f32[16]{0:T(128)} %dif_hbm.1, bf16[2,64,192]{2,1,0:T(8,128)(2,1)} %constant.4.clone.tab_hbm, ...), custom_call_target="tpu_custom_call" | custom-call | tf_op jit(solution)/shard_map/pallas_call | solution.py:671
  20.9 0.6 %copy.10 = f32[3,2,4,4,65]{4,3,2,1,0:T(4,128)} copy(f32[3,2,4,4,65]{4,3,2,1,0:T(4,128)S(1)} %bitcast.4) | data formatting | bytes 49920

commit v6 on v5

--- a/solution.py
+++ b/solution.py
@@ -282,9 +282,10 @@
         blocks = ref.at[pl.ds(0, count)]
         pltpu.make_async_copy(blocks, blocks, sem).wait()
 
-    def coef_copy(s):
-        group = [s in g for g in coef_groups].index(True)
-        if s in gained:
+    def coef_copy(s, group=None):
+        if group is None:
+            group = [s in g for g in coef_groups].index(True)
+        if group == len(coef_groups) - 1:
             return remote(coef_all.at[s - 1], coef_all.at[s], coef_send.at[0], coef_recv.at[group], (mate, row))
         return remote(coef_ref, coef_all.at[s], coef_send.at[0], coef_recv.at[group], (target(s), row))
 
@@ -313,8 +314,10 @@
             leg_copy(2 * delta + 1).start()
         leg_copy(1).start()
 
-    for s in direct:
-        coef_copy(s).start()
+    for dy in (1, 0):
+        coef_copy(upper_z * (2 + dy) + (1 - upper_z) * (6 + dy), group=1 + (1 - dy)).start()
+        coef_copy(upper_z * (6 + dy) + (1 - upper_z) * (2 + dy), group=1 + (1 - dy)).start()
+    coef_copy(1, group=2).start()
 
     @pl.when(has_far)
     def _():

time: 21.7 us -> 21.9 us (level)
  no operation moved by 1% of the time
where the time goes in v6:
time: 21.9 us; the launch traced here: 21.7 us
  Pallas kernels  21.1 us (96%)
  local copies, waits for them, and re-layouts  0.62 us (3%)
    pallas_call x1, Pallas kernels, fused(): pl.pallas_call(functools.partial(fused_kernel, n_ma, n_row, pairs, rows,...  21.1 us
    unnamed x1, local copies, waits for them, and re-layouts  0.62 us

profile of v6, /device:TPU:1, one launch (start us, length us, event | category | flops | bytes accessed | tf_op | source)
XLA Modules:
  0.0 21.7 jit_solution(14054864083993435760)
XLA Ops:
  0.0 21.1 %shard_map.82 = f32[24,4,65]{2,1,0:T(4,128)S(1)} custom-call(bf16[24,4,65]{2,1,0:T(4,128)(2,1)} %bitcast.6, bf16[24,4,65]{2,1,0:T(4,128)(2,1)} %bitcast.7, bf16[65,4,384]{2,1,0:T(4,128)(2,1)} %bitcast.5, s32[4]{0:T(128)} %order_hbm.1, f32[384]{0:T(512)} %weight_hbm.1, f32[16]{0:T(128)} %dif_hbm.1, bf16[2,64,192]{2,1,0:T(8,128)(2,1)} %constant.4.clone.tab_hbm, ...), custom_call_target="tpu_custom_call" | custom-call | tf_op jit(solution)/shard_map/pallas_call | solution.py:674
  21.1 0.6 %copy.10 = f32[3,2,4,4,65]{4,3,2,1,0:T(4,128)} copy(f32[3,2,4,4,65]{4,3,2,1,0:T(4,128)S(1)} %bitcast.4) | data formatting | bytes 49920
